TPU v7x, 256 devices: a whole 4x4x8 slice. The times are simulated.
256 devices in a mesh: dp: 4 (over x_lo, core), expert: 64 (over x_hi, y, z).
Axes of the slice: x: 4 (x_hi: 2, x_lo: 2; x = x_hi * 2 + x_lo), y: 4, z: 8, core: 2. Of those that a mesh axis runs over, the one named last changes fastest.
Arguments:
- tokens: bfloat16 [16384, 4096], P(('dp', 'expert')), may hold values from -6 to 6
- token_experts: int32 [16384, 8], P(('dp', 'expert')), may hold values from 0 to 63, all different within a row; in each aligned block of 64 rows (0 to 63, 64 to 127, ...) at most 12 rows name the same one
- hidden_grad: bfloat16 [16384, 8, 768], P(('dp', 'expert')), may hold values from -6 to 6
- held_expert: int32 [64], replicated, may hold values from 0 to 63, each once
- swap_mask: int32 [64], replicated, may hold values from 0 to 1, as said below
- weight: bfloat16 [64, 4096, 768], P('expert', 'dp'), may hold values from -0.09375 to 0.09375
- first_moment: float32 [64, 4096, 768], P('expert', 'dp'), may hold values from -81.4587 to 81.4587
- second_moment: float32 [64, 4096, 768], P('expert', 'dp'), may hold values from 20.48 to 204.8
Outputs:
- token_grad: bfloat16 [16384, 4096], P(('dp', 'expert'))
- adam_step: bfloat16 [64, 4096, 768], P('expert', 'dp')
Inputs may be any that keep to these rules, and one draw needn't show every extreme that they name: `token_experts`: in each aligned block of 64 rows (the tokens of one device) no expert is named by more than 12 rows, and in some blocks one is named by exactly 12; the ids of a row differ. `held_expert`: a permutation of the expert ids. swap_mask[p] equals swap_mask[p + 32] for p below 32, and exactly 8 such pairs are 1.
All inputs are finite; a program needn't handle non-finite values.
Results may differ from a plain program's by a relative error of at most 0.008.
Values may be sent and summed in bfloat16 or wider, within the bound.
No kernel may reach another device: no remote copies, remote signals or barrier semaphores. Data moves between devices by JAX's collectives and lax.ppermute only.
A program may use at most 128 MiB of HBM per device.

v0:
```python
import jax
import jax.numpy as jnp
from jax import lax
from jax.sharding import PartitionSpec as P


def passed_along(block, axis, distance):
    devices = range(lax.axis_size(axis))
    route = [((i - distance) % len(devices), i) for i in devices]
    return lax.ppermute(block, axis, route)


def lookup(table, index, lanes):
    return jnp.sum(jnp.where(index[:, None] == lanes[None, :], table[None, :], 0), axis=1)


def adam_direction(grad, first, second):
    first_new = 0.9 * first + 0.1 * grad
    second_new = 0.95 * second + 0.05 * grad * grad
    return (first_new / (jnp.sqrt(second_new) + 1e-08)).astype(jnp.bfloat16)


def body(
    tokens, token_experts, hidden_grad, held_expert, swap_mask, weight, first_moment, second_moment
):
    count_dev = lax.axis_size("expert")
    half_way = count_dev // 2
    here = lax.axis_index("expert")
    tok_dev, top = token_experts.shape
    width = tokens.shape[1]
    hidden = hidden_grad.shape[2]
    capacity = min(tok_dev, 3 * tok_dev * top // (2 * count_dev))
    lanes = jnp.arange(count_dev, dtype=jnp.int32)
    partner = (lanes + half_way) % count_dev
    moving_all = swap_mask == 1
    new_held = jnp.where(moving_all, lookup(held_expert, partner, lanes), held_expert)
    moving = jnp.sum(jnp.where(lanes == here, swap_mask, 0)) == 1
    got_weight = passed_along(weight, "expert", half_way)
    got_first, got_second = (
        passed_along(first_moment.astype(jnp.bfloat16), "expert", half_way).astype(
            first_moment.dtype
        ),
        passed_along(second_moment.astype(jnp.bfloat16), "expert", half_way).astype(
            second_moment.dtype
        ),
    )
    w_shard = jnp.where(moving, got_weight, weight)
    first = jnp.where(moving, got_first, first_moment)
    second = jnp.where(moving, got_second, second_moment)
    owner = jnp.sum(jnp.where(new_held[None, :] == lanes[:, None], lanes[None, :], 0), axis=1)
    full_w = lax.all_gather(w_shard, "dp", axis=1, tiled=True)[0]
    flat_ids = token_experts.reshape(-1)
    dest = lookup(owner, flat_ids, lanes)
    onehot = (dest[:, None] == lanes[None, :]).astype(jnp.int32)
    before = jnp.cumsum(onehot, axis=0) - onehot
    rank = jnp.sum(before * onehot, axis=1)
    slot = dest * capacity + rank
    routed = tok_dev * top
    table = (
        jnp.zeros((count_dev * capacity,), jnp.int32)
        .at[slot]
        .set(jnp.arange(routed, dtype=jnp.int32) + 1)
    )
    filled = table > 0
    source_row = jnp.maximum(table - 1, 0)
    send_x = jnp.where(filled[:, None], tokens[source_row // top], jnp.zeros((), tokens.dtype))
    send_g = jnp.where(
        filled[:, None],
        hidden_grad.reshape(routed, hidden)[source_row],
        jnp.zeros((), hidden_grad.dtype),
    )
    recv_x, recv_g = (
        lax.all_to_all(
            send_x.reshape(count_dev, capacity, width),
            "expert",
            split_axis=0,
            concat_axis=0,
            tiled=True,
        ),
        lax.all_to_all(
            send_g.reshape(count_dev, capacity, hidden),
            "expert",
            split_axis=0,
            concat_axis=0,
            tiled=True,
        ),
    )
    rows_x = recv_x.reshape(count_dev * capacity, width)
    rows_g = recv_g.reshape(count_dev * capacity, hidden)
    pre = jnp.dot(rows_x, full_w, preferred_element_type=jnp.float32)
    sig = jax.nn.sigmoid(pre)
    grad_pre = (rows_g.astype(jnp.float32) * sig * (1.0 + pre * (1.0 - sig))).astype(jnp.bfloat16)
    back_rows = lax.dot_general(
        grad_pre, full_w, (((1,), (1,)), ((), ())), preferred_element_type=jnp.float32
    ).astype(jnp.bfloat16)
    returned = lax.all_to_all(
        back_rows.reshape(count_dev, capacity, width),
        "expert",
        split_axis=0,
        concat_axis=0,
        tiled=True,
    )
    picked = returned.reshape(count_dev * capacity, width)[slot].reshape(tok_dev, top, width)
    token_grad = jnp.sum(picked.astype(jnp.float32), axis=1).astype(jnp.bfloat16)
    expert_grad = lax.psum_scatter(
        lax.dot_general(
            rows_x, grad_pre, (((0,), (0,)), ((), ())), preferred_element_type=jnp.float32
        ).astype(jnp.bfloat16),
        "dp",
        scatter_dimension=0,
        tiled=True,
    ).astype(jnp.float32)
    adam_step = adam_direction(expert_grad, first[0], second[0])[None]
    return (token_grad, adam_step)


def solution(mesh):
    in_specs = (
        P(("dp", "expert"), None),
        P(("dp", "expert"), None),
        P(("dp", "expert"), None, None),
        P(),
        P(),
        P("expert", "dp", None),
        P("expert", "dp", None),
        P("expert", "dp", None),
    )
    out_specs = (P(("dp", "expert"), None), P("expert", "dp", None))
    return jax.shard_map(body, mesh=mesh, in_specs=in_specs, out_specs=out_specs, check_vma=False)
```

profile of v0, /device:TPU:120, one launch (start us, length us, event | category | flops | bytes accessed | tf_op | source)
XLA Modules:
  0.0 552.8 jit_solution(5621771242300837301)
XLA Ops:
  14.8 2.8 gather_fusion
  19.2 13.0 %all-to-all-start = ((bf16[64,12,768]{2,1,0:T(8,128)(2,1)}), bf16[64,12,768]{2,1,0:T(8,128)(2,1)S(1)}, u32[]{:S(2)}, u32[]{:S(2)}) async-start(bf16[64,12,768]{2,1,0:T(8,128)(2,1)} %broadcast_select_fusion.2), calls=%async_computation | async-start | bytes 3145728 | tf_op jit(solution)/shard_map/all_to_all | solution.py:80
  32.3 5.7 %gather_fusion.1 = bf16[768,4096]{1,0:T(8,128)(2,1)} fusion(bf16[64,4096]{1,0:T(8,128)(2,1)S(1)} %copy-done.2, s32[1024]{0:T(1024)S(1)} %get-tuple-element.6), kind=kCustom, calls=%fused_computation.1 | custom fusion | bytes 12585984 | tf_op jit(solution)/shard_map/gather | solution.py:66
  38.0 9.7 %gather.16 = bf16[64,12,4096]{2,1,0:T(8,128)(2,1)} reshape(bf16[768,4096]{1,0:T(8,128)(2,1)} %gather_fusion.1) | data formatting | bytes 12582912 | tf_op jit(solution)/shard_map/gather | solution.py:66
  47.8 7.2 %broadcast_select_fusion = bf16[64,12,4096]{2,1,0:T(8,128)(2,1)} fusion(bf16[64,12,4096]{2,1,0:T(8,128)(2,1)} %gather.16, pred[64,12]{1,0:T(8,128)(4,1)S(1)} %broadcast_in_dim.83), kind=kLoop, calls=%fused_computation.4 | loop fusion | flops 3145728 | bytes 12583680 | tf_op jit(solution)/shard_map/jit(_where)/select_n | solution.py:66
  55.0 16.8 %all-to-all-done = bf16[64,12,768]{2,1,0:T(8,128)(2,1)S(1)} async-done(((bf16[64,12,768]{2,1,0:T(8,128)(2,1)}), bf16[64,12,768]{2,1,0:T(8,128)(2,1)S(1)}, u32[]{:S(2)}, u32[]{:S(2)}) %all-to-all-start) | async-done | bytes 1179680 | tf_op jit(solution)/shard_map/all_to_all | solution.py:80
  71.8 8.4 %all-to-all-start.1 = ((bf16[64,12,4096]{2,1,0:T(8,128)(2,1)}), bf16[64,12,4096]{2,1,0:T(8,128)(2,1)}, u32[]{:S(2)}, u32[]{:S(2)}) async-start(bf16[64,12,4096]{2,1,0:T(8,128)(2,1)} %broadcast_select_fusion), calls=%async_computation.1 | async-start | bytes 16777216 | tf_op jit(solution)/shard_map/all_to_all | solution.py:73
  80.2 3.5 collective-permute-start
  84.3 74.6 %collective-permute-done = bf16[1,1024,768]{2,1,0:T(8,128)(2,1)} collective-permute-done((bf16[1,1024,768]{2,1,0:T(8,128)(2,1)}, bf16[1,1024,768]{2,1,0:T(8,128)(2,1)}, u32[]{:S(2)}, u32[]{:S(2)}) %collective-permute-start) | collective-permute-done | bytes 1572896 | tf_op jit(solution)/shard_map/ppermute | solution.py:10
  158.9 2.7 broadcast_select_fusion.1
  163.2 101.8 %all-to-all-done.1 = bf16[64,12,4096]{2,1,0:T(8,128)(2,1)} async-done(((bf16[64,12,4096]{2,1,0:T(8,128)(2,1)}), bf16[64,12,4096]{2,1,0:T(8,128)(2,1)}, u32[]{:S(2)}, u32[]{:S(2)}) %all-to-all-start.1) | async-done | bytes 6291488 | tf_op jit(solution)/shard_map/all_to_all | solution.py:73
  265.0 10.0 %reshape.103 = bf16[768,4096]{1,0:T(8,128)(2,1)} reshape(bf16[64,12,4096]{2,1,0:T(8,128)(2,1)} %all-to-all-done.1) | data formatting | bytes 12582912 | tf_op jit(solution)/shard_map/reshape | solution.py:88
  275.0 9.1 %fusion.1 = f32[768,768]{1,0:T(8,128)S(1)} fusion(bf16[768,4096]{1,0:T(8,128)(2,1)} %reshape.103, bf16[1,4096,768]{2,1,0:T(8,128)(2,1)} %all-gather.2.cloned.1.call-done), kind=kOutput, calls=%fused_computation.8 | convolution fusion | flops 4831838208 | bytes 14942208 | tf_op jit(solution)/shard_map/dot_general | solution.py:90
  285.5 8.2 %convolution_convert_fusion.1 = bf16[768,4096]{1,0:T(8,128)(2,1)} fusion(bf16[1,4096,768]{2,1,0:T(8,128)(2,1)S(1)} %copy-done.5, f32[768,768]{1,0:T(8,128)S(1)} %fusion.1, f32[768,768]{1,0:T(8,128)S(1)} %copy-done.4), kind=kOutput, calls=%fused_computation.6 | convolution fusion | flops 4840292352 | bytes 17301504 | tf_op jit(solution)/shard_map/dot_general | solution.py:93
  293.7 9.7 %reshape.104 = bf16[64,12,4096]{2,1,0:T(8,128)(2,1)} reshape(bf16[768,4096]{1,0:T(8,128)(2,1)} %convolution_convert_fusion.1) | data formatting | bytes 12582912 | tf_op jit(solution)/shard_map/reshape | solution.py:97
  303.4 14.0 %all-to-all-start.2 = ((bf16[64,12,4096]{2,1,0:T(8,128)(2,1)}), bf16[64,12,4096]{2,1,0:T(8,128)(2,1)}, u32[]{:S(2)}, u32[]{:S(2)}) async-start(bf16[64,12,4096]{2,1,0:T(8,128)(2,1)} %reshape.104), calls=%async_computation.2 | async-start | bytes 16777216 | tf_op jit(solution)/shard_map/all_to_all | solution.py:96
  317.5 10.1 %convolution_convert_fusion = bf16[4096,768]{1,0:T(8,128)(2,1)} fusion(bf16[768,4096]{1,0:T(8,128)(2,1)} %reshape.103, f32[768,768]{1,0:T(8,128)} %copy-done.6, f32[768,768]{1,0:T(8,128)S(1)} %copy-done.4), kind=kOutput, calls=%fused_computation.5 | convolution fusion | flops 4840292352 | bytes 17301504 | tf_op jit(solution)/shard_map/dot_general | solution.py:106
  327.6 3.4 convert_element_type.48
  331.0 3.2 collective-permute-start.1
  335.8 175.0 %all-to-all-done.2 = bf16[64,12,4096]{2,1,0:T(8,128)(2,1)} async-done(((bf16[64,12,4096]{2,1,0:T(8,128)(2,1)}), bf16[64,12,4096]{2,1,0:T(8,128)(2,1)}, u32[]{:S(2)}, u32[]{:S(2)}) %all-to-all-start.2) | async-done | bytes 6291488 | tf_op jit(solution)/shard_map/all_to_all | solution.py:96
  510.8 9.9 %reshape.105 = bf16[768,4096]{1,0:T(8,128)(2,1)} reshape(bf16[64,12,4096]{2,1,0:T(8,128)(2,1)} %all-to-all-done.2) | data formatting | bytes 12582912 | tf_op jit(solution)/shard_map/reshape | solution.py:103
  520.7 12.2 %gather_fusion.2 = bf16[512,4096]{1,0:T(8,128)(2,1)} fusion(bf16[768,4096]{1,0:T(8,128)(2,1)} %reshape.105, s32[1024]{0:T(1024)S(1)} %pad_clamp_fusion), kind=kCustom, calls=%fused_computation.2 | custom fusion | bytes 8390656 | tf_op jit(solution)/shard_map/gather | solution.py:103
  532.8 5.8 %bitcast_reduce_fusion = bf16[64,4096]{1,0:T(8,128)(2,1)} fusion(bf16[512,4096]{1,0:T(8,128)(2,1)} %gather_fusion.2), kind=kLoop, calls=%fused_computation.11 | loop fusion | flops 1835008 | bytes 4718592 | tf_op jit(solution)/shard_map/reduce_sum | solution.py:104
  538.7 7.3 %fusion.9 = bf16[1,1024,768]{2,1,0:T(8,128)(2,1)} fusion(f32[1,1024,768]{2,1,0:T(8,128)} %param.15, bf16[1,1024,768]{2,1,0:T(8,128)(2,1)} %collective-permute-done.2, bf16[1024,768]{1,0:T(8,128)(2,1)} %reduce-scatter.2.cloned.1.call-done, f32[1,1024,768]{2,1,0:T(8,128)} %param.14, bf16[1,1024,768]{2,1,0:T(8,128)(2,1)S(1)} %collective-permute-done.1, pred[]{:T(512)S(6)} %eq.105), kind=kLoop, calls=%fused_computation.22 | loop fusion | flops 11796480 | bytes 12582913 | tf_op jit(solution)/shard_map/broadcast_in_dim | solution.py:113
  (49 shorter events, 13.9 us)
Async XLA Ops:
  7.2 7.6 %copy-start = (bf16[64,8,768]{2,1,0:T(8,128)(2,1)S(1)}, bf16[64,8,768]{2,1,0:T(8,128)(2,1)}, u32[]{:S(2)}) copy-start(bf16[64,8,768]{2,1,0:T(8,128)(2,1)} %param.10) | copy-start | bytes 2359300
  17.9 14.4 %copy-start.2 = (bf16[64,4096]{1,0:T(8,128)(2,1)S(1)}, bf16[64,4096]{1,0:T(8,128)(2,1)}, u32[]{:S(2)}) copy-start(bf16[64,4096]{1,0:T(8,128)(2,1)} %param.8) | copy-start | bytes 1572868
  19.2 52.6 %all-to-all-start = ((bf16[64,12,768]{2,1,0:T(8,128)(2,1)}), bf16[64,12,768]{2,1,0:T(8,128)(2,1)S(1)}, u32[]{:S(2)}, u32[]{:S(2)}) async-start(bf16[64,12,768]{2,1,0:T(8,128)(2,1)} %broadcast_select_fusion.2), calls=%async_computation | async-start | bytes 3145728 | tf_op jit(solution)/shard_map/all_to_all | solution.py:80
  71.8 193.2 %all-to-all-start.1 = ((bf16[64,12,4096]{2,1,0:T(8,128)(2,1)}), bf16[64,12,4096]{2,1,0:T(8,128)(2,1)}, u32[]{:S(2)}, u32[]{:S(2)}) async-start(bf16[64,12,4096]{2,1,0:T(8,128)(2,1)} %broadcast_select_fusion), calls=%async_computation.1 | async-start | bytes 16777216 | tf_op jit(solution)/shard_map/all_to_all | solution.py:73
  80.2 194.8 %all-gather.2.cloned.1.call-start = ((), (), s32[]{:S(2)}) async-start(), calls=%async_computation.4 | async-start | bytes 7864320 | tf_op jit(solution)/shard_map/all_gather | solution.py:51
  80.2 78.7 %collective-permute-start = (bf16[1,1024,768]{2,1,0:T(8,128)(2,1)}, bf16[1,1024,768]{2,1,0:T(8,128)(2,1)}, u32[]{:S(2)}, u32[]{:S(2)}) collective-permute-start(bf16[1,1024,768]{2,1,0:T(8,128)(2,1)} %param.13), channel_id=1, source_target_pairs={{32,0},{33,1},{34,2},{35,3},{36,4},{37,5},{38,6},{39,7},{40,8},{41... | collective-permute-start | bytes 4718600 | tf_op jit(solution)/shard_map/ppermute | solution.py:10
  275.0 10.5 %copy-start.4 = (f32[768,768]{1,0:T(8,128)S(1)}, f32[768,768]{1,0:T(8,128)}, u32[]{:S(2)}) copy-start(f32[768,768]{1,0:T(8,128)} %reshape.107) | copy-start | bytes 7077892
  275.0 10.5 %copy-start.5 = (bf16[1,4096,768]{2,1,0:T(8,128)(2,1)S(1)}, bf16[1,4096,768]{2,1,0:T(8,128)(2,1)}, u32[]{:S(2)}) copy-start(bf16[1,4096,768]{2,1,0:T(8,128)(2,1)} %all-gather.2.cloned.1.call-done) | copy-start | bytes 18874372
  284.1 1.4 copy-start.6
  303.4 207.4 %all-to-all-start.2 = ((bf16[64,12,4096]{2,1,0:T(8,128)(2,1)}), bf16[64,12,4096]{2,1,0:T(8,128)(2,1)}, u32[]{:S(2)}, u32[]{:S(2)}) async-start(bf16[64,12,4096]{2,1,0:T(8,128)(2,1)} %reshape.104), calls=%async_computation.2 | async-start | bytes 16777216 | tf_op jit(solution)/shard_map/all_to_all | solution.py:96
  317.5 221.2 %reduce-scatter.2.cloned.1.call-start = ((), (), s32[]{:S(2)}) async-start(), calls=%async_computation.5 | async-start | bytes 7864320 | tf_op jit(solution)/shard_map/reduce_scatter | solution.py:105
  327.6 6.5 %copy-start.3 = (f32[1,1024,768]{2,1,0:T(8,128)S(1)}, f32[1,1024,768]{2,1,0:T(8,128)}, u32[]{:S(2)}) copy-start(f32[1,1024,768]{2,1,0:T(8,128)} %param.15) | copy-start | bytes 9437188
  331.0 207.6 %collective-permute-start.1 = (bf16[1,1024,768]{2,1,0:T(8,128)(2,1)}, bf16[1,1024,768]{2,1,0:T(8,128)(2,1)S(1)}, u32[]{:S(2)}, u32[]{:S(2)}) collective-permute-start(bf16[1,1024,768]{2,1,0:T(8,128)(2,1)} %convert_element_type.48), channel_id=1, source_target_pairs={{32,0},{33,1},{34,2},{35,3},{36,4},{37,5},{38,6},{39,7},{40,8},{41... | collective-permute-start | bytes 4718600 | tf_op jit(solution)/shard_map/ppermute | solution.py:10
  335.5 203.2 %collective-permute-start.2 = (bf16[1,1024,768]{2,1,0:T(8,128)(2,1)}, bf16[1,1024,768]{2,1,0:T(8,128)(2,1)}, u32[]{:S(2)}, u32[]{:S(2)}) collective-permute-start(bf16[1,1024,768]{2,1,0:T(8,128)(2,1)} %convert_element_type.52), channel_id=1, source_target_pairs={{32,0},{33,1},{34,2},{35,3},{36,4},{37,5},{38,6},{39,7},{40,8},{41... | collective-permute-start | bytes 4718600 | tf_op jit(solution)/shard_map/ppermute | solution.py:10
  538.7 7.3 %copy-start.1 = (bf16[64,8,768]{2,1,0:T(8,128)(2,1)S(1)}, bf16[64,8,768]{2,1,0:T(8,128)(2,1)}, u32[]{:S(2)}) copy-start(bf16[64,8,768]{2,1,0:T(8,128)(2,1)} %param.10) | copy-start | bytes 2359300
Sparse Core Ops, SparseCore 0:
  161.8 111.0 all-gather.1
  327.8 187.8 reduce-scatter.1
where the time goes:
time: 554 us; the launch traced here: 553 us
  waiting for transfers between devices  368 us (66%)
  local copies, waits for them, and re-layouts  66.9 us (12%)
  starting transfers between devices  42.5 us (8%)
  other arithmetic  32.9 us (6%)
  matrix products  27.4 us (5%)
  between operations  14.9 us (3%)
    all_to_all x1, waiting for transfers between devices, body(): lax.all_to_all(back_rows.reshape(count_dev, capacity, width), 'expert', s...  175 us
    all_to_all x1, waiting for transfers between devices, body(): lax.all_to_all(send_x.reshape(count_dev, capacity, width), 'expert', spli...  102 us
    ppermute x3, waiting for transfers between devices, passed_along(): return lax.ppermute(block, axis, route)  74.6 us
    all_to_all x1, waiting for transfers between devices, body(): lax.all_to_all(send_g.reshape(count_dev, capacity, hidden), 'expert', spl...  16.8 us
    gather x2, local copies, waits for them, and re-layouts, body(): tokens[source_row // top]  15.5 us
    all_to_all x1, starting transfers between devices, body(): lax.all_to_all(back_rows.reshape(count_dev, capacity, width), 'expert', s...  14 us
    all_to_all x1, starting transfers between devices, body(): lax.all_to_all(send_g.reshape(count_dev, capacity, hidden), 'expert', spl...  13 us
    gather x1, local copies, waits for them, and re-layouts, body(): returned.reshape(count_dev * capacity, width)[slot]  12.2 us
  transfers between devices with their start and end apart: 8, of which 4 were waited for; matrix products, arithmetic and copies ran while one was open for 14% of the time, Pallas kernels for 0%

commit v1 on v0

v1 whole, which is shorter than its diff:
```python
import jax
import jax.numpy as jnp
from jax import lax
from jax.sharding import Mesh, PartitionSpec as P

CHUNKS = 2
SWAP_PARTS = 2


def adam_direction(grad, first, second):
    first_new = 0.9 * first + 0.1 * grad
    second_new = 0.95 * second + 0.05 * grad * grad
    return (first_new / (jnp.sqrt(second_new) + 1e-08)).astype(jnp.bfloat16)


def dot(a, b, contract=((1,), (0,))):
    return lax.dot_general(a, b, (contract, ((), ())), preferred_element_type=jnp.float32)


def flipped_groups(with_z):
    nz = 8 if with_z else 1
    return [
        [
            (((low ^ high) * 2 + high) * 4 + y) * nz + z
            for high in range(2)
            for y in range(4)
            for z in range(nz)
        ]
        for low in range(2)
    ]


def exchange_plane(block):
    return lax.all_to_all(
        block, ("xl", "xh", "y"), 0, 0, axis_index_groups=flipped_groups(False), tiled=True
    )


def exchange_all(block):
    return lax.all_to_all(
        block, ("xl", "xh", "y", "z"), 0, 0, axis_index_groups=flipped_groups(True), tiled=True
    )


def swapped(block, axis):
    return lax.ppermute(block, axis, [(0, 1), (1, 0)])


def step(
    tokens, token_experts, hidden_grad, held_expert, swap_mask, weight, first_moment, second_moment
):
    bf16, f32, i32 = jnp.bfloat16, jnp.float32, jnp.int32
    xl, core, xh = lax.axis_index("xl"), lax.axis_index("core"), lax.axis_index("xh")
    y, z = lax.axis_index("y"), lax.axis_index("z")
    here = (xh * 4 + y) * 8 + z
    tok_dev, top = token_experts.shape
    width, hidden = tokens.shape[1], hidden_grad.shape[2]
    slots = held_expert.shape[0]
    cap = 12
    planes, lanes_of_plane = 8, 8
    col = planes * tok_dev
    block = planes * cap
    rows = lanes_of_plane * block
    part = width // CHUNKS

    w_own = weight[0]
    w_x = swapped(w_own, "xl")
    w_c = swapped(w_own, "core")
    w_xc = swapped(w_x, "core")
    me = xl * 2 + core
    shard = w_own.shape[0]
    full_w = jnp.zeros((width, hidden), bf16)
    for piece, at in ((w_own, me), (w_c, me ^ 1), (w_x, me ^ 2), (w_xc, me ^ 3)):
        full_w = lax.dynamic_update_slice(full_w, piece, (at * shard, 0))

    same = token_experts[:, :, None] == held_expert[None, None, :]
    named = jnp.sum(same.astype(f32), axis=1).astype(bf16)
    earlier = (
        lax.broadcasted_iota(i32, (tok_dev, tok_dev), 1)
        < lax.broadcasted_iota(i32, (tok_dev, tok_dev), 0)
    ).astype(bf16)
    rank = named.astype(f32) * (dot(earlier, named) + 1.0)

    marks = jnp.pad(rank.astype(bf16), ((0, 0), (0, 128 - slots)))
    gathered = []
    for c in range(CHUNKS):
        piece = tokens[:, c * part : (c + 1) * part]
        if c == 0:
            piece = jnp.concatenate([piece, marks], axis=1)
        gathered.append(lax.all_gather(piece, "z", axis=0, tiled=True))

    place = jnp.arange(slots, dtype=f32) * cap - 1.0
    slot = jnp.sum(jnp.where(same, (rank + place[None, :])[:, None, :], 0.0), axis=2)
    slot = slot.astype(i32).reshape(1, tok_dev * top)
    pick_g = (lax.broadcasted_iota(i32, (slots * cap, tok_dev * top), 0) == slot).astype(bf16)
    send_g = dot(pick_g, hidden_grad.reshape(tok_dev * top, hidden)).astype(bf16)
    rows_g = exchange_all(send_g.reshape(slots, cap, hidden))
    rows_g = rows_g.reshape(rows, hidden)

    marks_col = gathered[0][:, part : part + slots]
    lane_i = lax.broadcasted_iota(i32, (lanes_of_plane, slots), 0)
    slot_i = lax.broadcasted_iota(i32, (lanes_of_plane, slots), 1)
    choose = (slot_i == lane_i * planes + z).astype(bf16)
    value = dot(choose, marks_col, ((1,), (1,))).astype(i32)
    q = lax.broadcasted_iota(i32, (block, col), 0)
    t = lax.broadcasted_iota(i32, (block, col), 1)
    wanted = jnp.where(q // cap == t // tok_dev, q % cap + 1, -1)
    pick = (value[:, None, :] == wanted[None, :, :]).astype(bf16).reshape(rows, col)

    xs = []
    for c in range(CHUNKS):
        sent = dot(pick, gathered[c][:, :part]).astype(bf16)
        got = exchange_plane(sent.reshape(lanes_of_plane, block, part))
        xs.append(got.reshape(rows, part))
    pre = dot(xs[0], full_w[:part])
    for c in range(1, CHUNKS):
        pre = pre + dot(xs[c], full_w[c * part : (c + 1) * part])
    sig = jax.nn.sigmoid(pre)
    grad_pre = (rows_g.astype(f32) * sig * (1.0 + pre * (1.0 - sig))).astype(bf16)

    grads = []
    for c in range(CHUNKS):
        back = dot(grad_pre, full_w[c * part : (c + 1) * part], ((1,), (1,))).astype(bf16)
        back = exchange_plane(back.reshape(lanes_of_plane, block, part))
        summed = dot(pick, back.reshape(rows, part), ((0,), (0,))).astype(bf16)
        grads.append(lax.psum_scatter(summed, "z", scatter_dimension=0, tiled=True))
    token_grad = jnp.concatenate(grads, axis=1)

    dw = jnp.concatenate([dot(x, grad_pre, ((0,), (0,))).astype(bf16) for x in xs], axis=0)
    dw = dw.reshape(2, 2, shard, hidden)
    to_core = lax.dynamic_slice_in_dim(dw, 1 - core, 1, axis=1)[:, 0]
    kept = lax.dynamic_slice_in_dim(dw, core, 1, axis=1)[:, 0]
    both = kept.astype(f32) + swapped(to_core, "core").astype(f32)
    mine = lax.dynamic_slice_in_dim(both, xl, 1, axis=0)[0]
    other = lax.dynamic_slice_in_dim(both, 1 - xl, 1, axis=0)[0].astype(bf16)
    moving = jnp.sum(jnp.where(jnp.arange(slots, dtype=i32) == here, swap_mask, 0)) == 1
    size = shard // SWAP_PARTS
    steps = []
    for s in range(SWAP_PARTS):
        at = slice(s * size, (s + 1) * size)
        grad = mine[at] + swapped(other[at], "xl").astype(f32)
        step = adam_direction(grad, first_moment[0, at], second_moment[0, at])
        steps.append(jnp.where(moving, swapped(step, "xh"), step))
    adam_step = jnp.concatenate(steps, axis=0)[None]
    return (token_grad, adam_step)


def solution(mesh):
    names = ("xl", "core", "xh", "y", "z")
    fine = Mesh(mesh.devices.reshape(2, 2, 2, 4, 8), names)
    dp, expert = ("xl", "core"), ("xh", "y", "z")
    in_specs = (
        P(names, None),
        P(names, None),
        P(names, None, None),
        P(),
        P(),
        P(expert, dp, None),
        P(expert, dp, None),
        P(expert, dp, None),
    )
    out_specs = (P(names, None), P(expert, dp, None))
    return jax.shard_map(step, mesh=fine, in_specs=in_specs, out_specs=out_specs, check_vma=False)
```

time: 554 us -> 411 us (0.74)
  waiting for transfers between devices: 368 us -> 247 us
  local copies, waits for them, and re-layouts: 66.9 us -> 24.1 us
  matrix products: 27.4 us -> 60.7 us
  other arithmetic: 32.9 us -> 18.4 us
    all_to_all x3 -> x5, waiting for transfers between devices: 294 us -> 88.1 us  [the longest x4 88.1 us: exchange_plane(): lax.all_to_all(block, ('xl', 'xh', 'y'), 0, 0, axis_index_groups=flipped_...]
    all_gather x1 -> x2, waiting for transfers between devices: 0.01 us -> 94.2 us  [step(): gathered.append(lax.all_gather(piece, 'z', axis=0, tiled=True))]
    dot_general x3 -> x13, matrix products: 27.4 us -> 60.7 us  [dot(): lax.dot_general(a, b, (contract, ((), ())), preferred_element_type=jnp.fl...]
    gather x5 -> x0, local copies, waits for them, and re-layouts: 30.7 us -> none  [the longest x2 15.5 us: body(): tokens[source_row // top]]
    reshape x3 -> x1, local copies, waits for them, and re-layouts: 29.6 us -> 1.29 us  [step(): rows_g = exchange_all(send_g.reshape(slots, cap, hidden))]
    select_n x6 -> x3, other arithmetic: 12.6 us -> 0.31 us  [the longest x2 0.17 us: step(): steps.append(jnp.where(moving, swapped(step, 'xh'), step))]
    ppermute x3 -> x8, waiting for transfers between devices: 74.6 us -> 64.4 us  [swapped(): return lax.ppermute(block, axis, [(0, 1), (1, 0)])]
    dynamic_update_slice x0 -> x4, local copies, waits for them, and re-layouts: none -> 9.33 us  [step(): full_w = lax.dynamic_update_slice(full_w, piece, (at * shard, 0))]
  transfers between devices with their start and end apart: 8 -> 17, of which waited for: 4 -> 10; matrix products, arithmetic and copies ran while one was open for 14% -> 20% of each run, Pallas kernels for 0% -> 0%
where the time goes in v1:
time: 411 us; the launch traced here: 407 us
  waiting for transfers between devices  247 us (60%)
  matrix products  60.7 us (15%)
  starting transfers between devices  41.7 us (10%)
  local copies, waits for them, and re-layouts  24.1 us (6%)
  other arithmetic  18.4 us (4%)
  between operations  14.6 us (4%)
    all_gather x2, waiting for transfers between devices, step(): gathered.append(lax.all_gather(piece, 'z', axis=0, tiled=True))  94.2 us
    all_to_all x4, waiting for transfers between devices, exchange_plane(): lax.all_to_all(block, ('xl', 'xh', 'y'), 0, 0, axis_index_groups=flipped_...  88.1 us
    ppermute x8, waiting for transfers between devices, swapped(): return lax.ppermute(block, axis, [(0, 1), (1, 0)])  64.4 us
    dot_general x13, matrix products, dot(): lax.dot_general(a, b, (contract, ((), ())), preferred_element_type=jnp.fl...  60.7 us
    all_to_all x4, starting transfers between devices, exchange_plane(): lax.all_to_all(block, ('xl', 'xh', 'y'), 0, 0, axis_index_groups=flipped_...  22.4 us
    all_to_all x1, starting transfers between devices, exchange_all(): lax.all_to_all(block, ('xl', 'xh', 'y', 'z'), 0, 0, axis_index_groups=fli...  12.8 us
    dynamic_update_slice x4, local copies, waits for them, and re-layouts, step(): full_w = lax.dynamic_update_slice(full_w, piece, (at * shard, 0))  9.33 us
  transfers between devices with their start and end apart: 17, of which 10 were waited for; matrix products, arithmetic and copies ran while one was open for 20% of the time, Pallas kernels for 0%

profile of v1, /device:TPU:120, one launch (start us, length us, event | category | flops | bytes accessed | tf_op | source)
XLA Modules:
  0.0 406.9 jit_solution(3979186709092047416)
XLA Ops:
  15.4 12.8 %all-to-all-start = ((bf16[64,12,768]{2,1,0:T(8,128)(2,1)}), bf16[64,12,768]{2,1,0:T(8,128)(2,1)S(1)}, u32[]{:S(2)}, u32[]{:S(2)}) async-start(bf16[64,12,768]{2,1,0:T(8,128)(2,1)} %reshape.184), calls=%async_computation | async-start | bytes 3145728 | tf_op jit(solution)/shard_map/all_to_all | solution.py:40
  28.4 54.3 %all-gather.3.cloned.1.call-done = bf16[512,2176]{1,0:T(8,128)(2,1)} async-done(((bf16[64,2176]{1,0:T(8,128)(2,1)}), bf16[512,2176]{1,0:T(8,128)(2,1)}) %all-gather.3.cloned.1.call-update) | async-done | bytes 2228240 | tf_op jit(solution)/shard_map/all_gather | solution.py:90
  84.1 39.8 %all-gather.5.cloned.1.call-done = bf16[512,2048]{1,0:T(8,128)(2,1)} async-done(((bf16[64,2048]{1,0:T(8,128)(2,1)}), bf16[512,2048]{1,0:T(8,128)(2,1)}) %all-gather.5.cloned.1.call-update) | async-done | bytes 2097168 | tf_op jit(solution)/shard_map/all_gather | solution.py:90
  128.9 6.9 %all-to-all-start.2 = ((bf16[8,96,2048]{2,1,0:T(8,128)(2,1)}), bf16[8,96,2048]{2,1,0:T(8,128)(2,1)}, u32[]{:S(2)}, u32[]{:S(2)}) async-start(bf16[8,96,2048]{2,1,0:T(8,128)(2,1)} %bitcast.84), calls=%async_computation.2 | async-start | bytes 6291456 | tf_op jit(solution)/shard_map/all_to_all | solution.py:34
  141.1 27.1 %all-to-all-done.2 = bf16[8,96,2048]{2,1,0:T(8,128)(2,1)} async-done(((bf16[8,96,2048]{2,1,0:T(8,128)(2,1)}), bf16[8,96,2048]{2,1,0:T(8,128)(2,1)}, u32[]{:S(2)}, u32[]{:S(2)}) %all-to-all-start.2) | async-done | bytes 3145760 | tf_op jit(solution)/shard_map/all_to_all | solution.py:34
  168.2 5.3 %all-to-all-start.1 = ((bf16[8,96,2048]{2,1,0:T(8,128)(2,1)}), bf16[8,96,2048]{2,1,0:T(8,128)(2,1)}, u32[]{:S(2)}, u32[]{:S(2)}) async-start(bf16[8,96,2048]{2,1,0:T(8,128)(2,1)} %bitcast.82), calls=%async_computation.1 | async-start | bytes 6291456 | tf_op jit(solution)/shard_map/all_to_all | solution.py:34
  188.0 7.0 %fusion.1 = f32[768,768]{1,0:T(8,128)} fusion(bf16[768,2048]{1,0:T(8,128)(2,1)} %bitcast.6, bf16[4096,768]{1,0:T(8,128)(2,1)} %constant_dynamic-update-slice_fusion), kind=kOutput, calls=%fused_computation.13 | convolution fusion | flops 2415919104 | bytes 8650752 | tf_op jit(solution)/shard_map/dot_general | solution.py:17
  194.9 15.8 %all-to-all-done.1 = bf16[8,96,2048]{2,1,0:T(8,128)(2,1)} async-done(((bf16[8,96,2048]{2,1,0:T(8,128)(2,1)}), bf16[8,96,2048]{2,1,0:T(8,128)(2,1)}, u32[]{:S(2)}, u32[]{:S(2)}) %all-to-all-start.1) | async-done | bytes 3145760 | tf_op jit(solution)/shard_map/all_to_all | solution.py:34
  210.7 6.6 %multiply_convert_fusion = bf16[768,768]{1,0:T(8,128)(2,1)S(1)} fusion(f32[768,768]{1,0:T(8,128)S(1)} %copy-done.5, f32[768,768]{1,0:T(8,128)} %fusion.1, bf16[768,2048]{1,0:T(8,128)(2,1)} %bitcast.3, bf16[4096,768]{1,0:T(8,128)(2,1)} %constant_dynamic-update-slice_fusion), kind=kOutput, calls=%fused_computation.20 | convolution fusion | flops 2421817344 | bytes 12189696 | tf_op jit(solution)/shard_map/dot_general | solution.py:17
  217.4 6.4 %convolution_convert_fusion.2 = bf16[768,2048]{1,0:T(8,128)(2,1)} fusion(bf16[768,768]{1,0:T(8,128)(2,1)S(1)} %multiply_convert_fusion, bf16[4096,768]{1,0:T(8,128)(2,1)} %constant_dynamic-update-slice_fusion), kind=kOutput, calls=%fused_computation.6 | convolution fusion | flops 2417491968 | bytes 7471104 | tf_op jit(solution)/shard_map/dot_general | solution.py:17
  223.7 5.2 %all-to-all-start.4 = ((bf16[8,96,2048]{2,1,0:T(8,128)(2,1)}), bf16[8,96,2048]{2,1,0:T(8,128)(2,1)}, u32[]{:S(2)}, u32[]{:S(2)}) async-start(bf16[8,96,2048]{2,1,0:T(8,128)(2,1)} %bitcast.85), calls=%async_computation.5 | async-start | bytes 6291456 | tf_op jit(solution)/shard_map/all_to_all | solution.py:34
  228.9 5.9 %convolution_convert_fusion.3 = bf16[768,2048]{1,0:T(8,128)(2,1)} fusion(bf16[768,768]{1,0:T(8,128)(2,1)S(1)} %copy-done.9, bf16[4096,768]{1,0:T(8,128)(2,1)} %constant_dynamic-update-slice_fusion), kind=kOutput, calls=%fused_computation.7 | convolution fusion | flops 2417491968 | bytes 7471104 | tf_op jit(solution)/shard_map/dot_general | solution.py:17
  234.8 6.2 %convolution_convert_fusion = bf16[2048,768]{1,0:T(8,128)(2,1)} fusion(bf16[768,2048]{1,0:T(8,128)(2,1)} %bitcast.6, bf16[768,768]{1,0:T(8,128)(2,1)S(1)} %copy-done.9), kind=kOutput, calls=%fused_computation.4 | convolution fusion | flops 2417491968 | bytes 7471104 | tf_op jit(solution)/shard_map/dot_general | solution.py:17
  241.0 25.3 %all-to-all-done.4 = bf16[8,96,2048]{2,1,0:T(8,128)(2,1)} async-done(((bf16[8,96,2048]{2,1,0:T(8,128)(2,1)}), bf16[8,96,2048]{2,1,0:T(8,128)(2,1)}, u32[]{:S(2)}, u32[]{:S(2)}) %all-to-all-start.4) | async-done | bytes 3145760 | tf_op jit(solution)/shard_map/all_to_all | solution.py:34
  266.3 5.0 %all-to-all-start.3 = ((bf16[8,96,2048]{2,1,0:T(8,128)(2,1)}), bf16[8,96,2048]{2,1,0:T(8,128)(2,1)}, u32[]{:S(2)}, u32[]{:S(2)}) async-start(bf16[8,96,2048]{2,1,0:T(8,128)(2,1)} %bitcast.83), calls=%async_computation.3 | async-start | bytes 6291456 | tf_op jit(solution)/shard_map/all_to_all | solution.py:34
  271.3 5.0 %bitcast_convert_fusion = bf16[512,2048]{1,0:T(8,128)(2,1)} fusion(bf16[8,96,2048]{2,1,0:T(8,128)(2,1)} %all-to-all-done.4, s32[96,512]{1,0:T(8,128)S(1)} %add_select_fusion, s32[8,512]{1,0:T(8,128)S(1)} %convolution_convert_fusion.6), kind=kOutput, calls=%fused_computation.2 | convolution fusion | flops 1612054528 | bytes 5455872 | tf_op jit(solution)/shard_map/dot_general | solution.py:17
  276.4 6.4 %convolution_convert_fusion.1 = bf16[2048,768]{1,0:T(8,128)(2,1)} fusion(bf16[768,2048]{1,0:T(8,128)(2,1)} %bitcast.3, bf16[768,768]{1,0:T(8,128)(2,1)S(1)} %copy-done.9), kind=kOutput, calls=%fused_computation.5 | convolution fusion | flops 2417491968 | bytes 7471104 | tf_op jit(solution)/shard_map/dot_general | solution.py:17
  288.7 19.9 %all-to-all-done.3 = bf16[8,96,2048]{2,1,0:T(8,128)(2,1)} async-done(((bf16[8,96,2048]{2,1,0:T(8,128)(2,1)}), bf16[8,96,2048]{2,1,0:T(8,128)(2,1)}, u32[]{:S(2)}, u32[]{:S(2)}) %all-to-all-start.3) | async-done | bytes 3145760 | tf_op jit(solution)/shard_map/all_to_all | solution.py:34
  308.7 5.1 %bitcast_convert_fusion.1 = bf16[512,2048]{1,0:T(8,128)(2,1)} fusion(bf16[8,96,2048]{2,1,0:T(8,128)(2,1)} %all-to-all-done.3, s32[96,512]{1,0:T(8,128)S(1)} %add_select_fusion, s32[8,512]{1,0:T(8,128)S(1)} %convolution_convert_fusion.6), kind=kOutput, calls=%fused_computation.3 | convolution fusion | flops 1612054528 | bytes 5455872 | tf_op jit(solution)/shard_map/dot_general | solution.py:17
  322.1 18.4 %collective-permute-done.4 = bf16[512,768]{1,0:T(8,128)(2,1)S(1)} collective-permute-done((bf16[512,768]{1,0:T(8,128)(2,1)S(1)}, bf16[512,768]{1,0:T(8,128)(2,1)S(1)}, u32[]{:S(2)}, u32[]{:S(2)}) %collective-permute-start.4) | collective-permute-done | bytes 786464 | tf_op jit(solution)/shard_map/ppermute | solution.py:46
  340.4 14.7 %collective-permute-done.6 = bf16[512,768]{1,0:T(8,128)(2,1)S(1)} collective-permute-done((bf16[512,768]{1,0:T(8,128)(2,1)S(1)}, bf16[512,768]{1,0:T(8,128)(2,1)S(1)}, u32[]{:S(2)}, u32[]{:S(2)}) %collective-permute-start.6) | collective-permute-done | bytes 786464 | tf_op jit(solution)/shard_map/ppermute | solution.py:46
  355.2 5.8 %fusion.18 = (bf16[512,768]{1,0:T(8,128)(2,1)S(1)}, bf16[512,768]{1,0:T(8,128)(2,1)S(1)}) fusion(f32[1,1024,768]{2,1,0:T(8,128)} %param.15, bf16[512,768]{1,0:T(8,128)(2,1)S(1)} %collective-permute-done.4, f32[2,1024,768]{2,1,0:T(8,128)} %copy-done.3, s32[]{:T(128)S(6)} %select_n.92, f32[1,1024,768]{2,1,0:T(8,128)} %param.14, ...), kind=kLoop, calls=%fused_computation.39 | loop fusion | flops 9437184 | bytes 12582920 | tf_op jit(solution)/shard_map/convert_element_type | solution.py:13
  365.8 17.1 %collective-permute-done.7 = bf16[512,768]{1,0:T(8,128)(2,1)S(1)} collective-permute-done((bf16[512,768]{1,0:T(8,128)(2,1)S(1)}, bf16[512,768]{1,0:T(8,128)(2,1)S(1)}, u32[]{:S(2)}, u32[]{:S(2)}) %collective-permute-start.7) | collective-permute-done | bytes 786464 | tf_op jit(solution)/shard_map/ppermute | solution.py:46
  383.0 14.1 %collective-permute-done.5 = bf16[512,768]{1,0:T(8,128)(2,1)S(1)} collective-permute-done((bf16[512,768]{1,0:T(8,128)(2,1)S(1)}, bf16[512,768]{1,0:T(8,128)(2,1)S(1)}, u32[]{:S(2)}, u32[]{:S(2)}) %collective-permute-start.5) | collective-permute-done | bytes 786464 | tf_op jit(solution)/shard_map/ppermute | solution.py:46
  (81 shorter events, 56.1 us)
Async XLA Ops:
  7.2 6.1 %copy-start = (bf16[64,8,768]{2,1,0:T(8,128)(2,1)S(1)}, bf16[64,8,768]{2,1,0:T(8,128)(2,1)}, u32[]{:S(2)}) copy-start(bf16[64,8,768]{2,1,0:T(8,128)(2,1)} %param.10) | copy-start | bytes 2359300
  7.2 75.6 %all-gather.3.cloned.1.call-start = ((), (), s32[]{:S(2)}) async-start(), calls=%async_computation.7 | async-start | bytes 2506752 | tf_op jit(solution)/shard_map/all_gather | solution.py:90
  11.5 112.4 %all-gather.5.cloned.1.call-start = ((), (), s32[]{:S(2)}) async-start(), calls=%async_computation.8 | async-start | bytes 2359296 | tf_op jit(solution)/shard_map/all_gather | solution.py:90
  15.4 113.5 %all-to-all-start = ((bf16[64,12,768]{2,1,0:T(8,128)(2,1)}), bf16[64,12,768]{2,1,0:T(8,128)(2,1)S(1)}, u32[]{:S(2)}, u32[]{:S(2)}) async-start(bf16[64,12,768]{2,1,0:T(8,128)(2,1)} %reshape.184), calls=%async_computation | async-start | bytes 3145728 | tf_op jit(solution)/shard_map/all_to_all | solution.py:40
  128.9 39.3 %all-to-all-start.2 = ((bf16[8,96,2048]{2,1,0:T(8,128)(2,1)}), bf16[8,96,2048]{2,1,0:T(8,128)(2,1)}, u32[]{:S(2)}, u32[]{:S(2)}) async-start(bf16[8,96,2048]{2,1,0:T(8,128)(2,1)} %bitcast.84), calls=%async_computation.2 | async-start | bytes 6291456 | tf_op jit(solution)/shard_map/all_to_all | solution.py:34
  135.8 37.7 %collective-permute-start.1 = (bf16[1024,768]{1,0:T(8,128)(2,1)}, bf16[1024,768]{1,0:T(8,128)(2,1)}, u32[]{:S(2)}, u32[]{:S(2)}) collective-permute-start(bf16[1024,768]{1,0:T(8,128)(2,1)} %bitcast.86), channel_id=1, source_target_pairs={{0,128},{128,0},{1,129},{129,1},{2,130},{130,2},{3,131},{131,3},{4... | collective-permute-start | bytes 4718600 | tf_op jit(solution)/shard_map/ppermute | solution.py:46
  168.2 42.5 %all-to-all-start.1 = ((bf16[8,96,2048]{2,1,0:T(8,128)(2,1)}), bf16[8,96,2048]{2,1,0:T(8,128)(2,1)}, u32[]{:S(2)}, u32[]{:S(2)}) async-start(bf16[8,96,2048]{2,1,0:T(8,128)(2,1)} %bitcast.82), calls=%async_computation.1 | async-start | bytes 6291456 | tf_op jit(solution)/shard_map/all_to_all | solution.py:34
  173.5 4.9 %collective-permute-start = (bf16[1024,768]{1,0:T(8,128)(2,1)}, bf16[1024,768]{1,0:T(8,128)(2,1)}, u32[]{:S(2)}, u32[]{:S(2)}) collective-permute-start(bf16[1024,768]{1,0:T(8,128)(2,1)} %bitcast.87), channel_id=1, source_target_pairs={{0,64},{64,0},{1,65},{65,1},{2,66},{66,2},{3,67},{67,3},{4,68},{68... | collective-permute-start | bytes 4718600 | tf_op jit(solution)/shard_map/ppermute | solution.py:46
  173.5 11.7 %collective-permute-start.2 = (bf16[1024,768]{1,0:T(8,128)(2,1)}, bf16[1024,768]{1,0:T(8,128)(2,1)}, u32[]{:S(2)}, u32[]{:S(2)}) collective-permute-start(bf16[1024,768]{1,0:T(8,128)(2,1)} %collective-permute-done.1), channel_id=1, source_target_pairs={{0,64},{64,0},{1,65},{65,1},{2,66},{66,2},{3,67},{67,3},{4,68},{68... | collective-permute-start | bytes 4718600 | tf_op jit(solution)/shard_map/ppermute | solution.py:46
  188.0 22.7 %copy-start.5 = (f32[768,768]{1,0:T(8,128)S(1)}, f32[768,768]{1,0:T(8,128)}, u32[]{:S(2)}) copy-start(f32[768,768]{1,0:T(8,128)} %reshape.192) | copy-start | bytes 7077892
  217.4 6.4 %copy-start.8 = (bf16[768,768]{1,0:T(8,128)(2,1)}, bf16[768,768]{1,0:T(8,128)(2,1)S(1)}, u32[]{:S(2)}) copy-start(bf16[768,768]{1,0:T(8,128)(2,1)S(1)} %multiply_convert_fusion) | copy-start | bytes 3538948
  223.7 5.2 %copy-start.9 = (bf16[768,768]{1,0:T(8,128)(2,1)S(1)}, bf16[768,768]{1,0:T(8,128)(2,1)}, u32[]{:S(2)}) copy-start(bf16[768,768]{1,0:T(8,128)(2,1)} %copy-done.8) | copy-start | bytes 3538948
  223.7 42.5 %all-to-all-start.4 = ((bf16[8,96,2048]{2,1,0:T(8,128)(2,1)}), bf16[8,96,2048]{2,1,0:T(8,128)(2,1)}, u32[]{:S(2)}, u32[]{:S(2)}) async-start(bf16[8,96,2048]{2,1,0:T(8,128)(2,1)} %bitcast.85), calls=%async_computation.5 | async-start | bytes 6291456 | tf_op jit(solution)/shard_map/all_to_all | solution.py:34
  266.3 42.4 %all-to-all-start.3 = ((bf16[8,96,2048]{2,1,0:T(8,128)(2,1)}), bf16[8,96,2048]{2,1,0:T(8,128)(2,1)}, u32[]{:S(2)}, u32[]{:S(2)}) async-start(bf16[8,96,2048]{2,1,0:T(8,128)(2,1)} %bitcast.83), calls=%async_computation.3 | async-start | bytes 6291456 | tf_op jit(solution)/shard_map/all_to_all | solution.py:34
  271.3 127.2 %reduce-scatter.5.cloned.1.call-start = ((), (), s32[]{:S(2)}) async-start(), calls=%async_computation.10 | async-start | bytes 2359296 | tf_op jit(solution)/shard_map/reduce_scatter | solution.py:126
  276.4 122.1 %reduce-scatter.3.cloned.1.call-start = ((), (), s32[]{:S(2)}) async-start(), calls=%async_computation.9 | async-start | bytes 2359296 | tf_op jit(solution)/shard_map/reduce_scatter | solution.py:126
  276.4 6.4 %copy-start.4 = (bf16[2048,768]{1,0:T(8,128)(2,1)S(1)}, bf16[2048,768]{1,0:T(8,128)(2,1)}, u32[]{:S(2)}) copy-start(bf16[2048,768]{1,0:T(8,128)(2,1)} %convolution_convert_fusion) | copy-start | bytes 9437188
  285.2 3.6 copy-start.2
  288.7 25.1 %collective-permute-start.3 = (bf16[2,1024,768]{2,1,0:T(8,128)(2,1)}, bf16[2,1024,768]{2,1,0:T(8,128)(2,1)}, u32[]{:S(2)}, u32[]{:S(2)}) collective-permute-start(bf16[2,1024,768]{2,1,0:T(8,128)(2,1)} %dynamic-slice_bitcast_fusion), channel_id=1, source_target_pairs={{0,64},{64,0},{1,65},{65,1},{2,66},{66,2},{3,67},{67,3},{4,68},{68... | collective-permute-start | bytes 9437192 | tf_op jit(solution)/shard_map/ppermute | solution.py:46
  320.0 20.4 %collective-permute-start.4 = (bf16[512,768]{1,0:T(8,128)(2,1)S(1)}, bf16[512,768]{1,0:T(8,128)(2,1)S(1)}, u32[]{:S(2)}, u32[]{:S(2)}) collective-permute-start(bf16[512,768]{1,0:T(8,128)(2,1)S(1)} %get-tuple-element.4), channel_id=1, source_target_pairs={{0,128},{128,0},{1,129},{129,1},{2,130},{130,2},{3,131},{131,3},{4... | collective-permute-start | bytes 2359304 | tf_op jit(solution)/shard_map/ppermute | solution.py:46
  320.0 35.1 %collective-permute-start.6 = (bf16[512,768]{1,0:T(8,128)(2,1)S(1)}, bf16[512,768]{1,0:T(8,128)(2,1)S(1)}, u32[]{:S(2)}, u32[]{:S(2)}) collective-permute-start(bf16[512,768]{1,0:T(8,128)(2,1)S(1)} %get-tuple-element.5), channel_id=1, source_target_pairs={{0,128},{128,0},{1,129},{129,1},{2,130},{130,2},{3,131},{131,3},{4... | collective-permute-start | bytes 2359304 | tf_op jit(solution)/shard_map/ppermute | solution.py:46
  322.1 42.5 %copy-start.7 = (s32[64]{0:T(128)S(1)}, s32[64]{0:T(128)}, u32[]{:S(2)}) copy-start(s32[64]{0:T(128)} %param.12) | copy-start | bytes 772
  360.9 22.0 %collective-permute-start.7 = (bf16[512,768]{1,0:T(8,128)(2,1)S(1)}, bf16[512,768]{1,0:T(8,128)(2,1)S(1)}, u32[]{:S(2)}, u32[]{:S(2)}) collective-permute-start(bf16[512,768]{1,0:T(8,128)(2,1)S(1)} %get-tuple-element.3), channel_id=1, source_target_pairs={{0,32},{32,0},{1,33},{33,1},{2,34},{34,2},{3,35},{35,3},{4,36},{36... | collective-permute-start | bytes 2359304 | tf_op jit(solution)/shard_map/ppermute | solution.py:46
  363.0 34.2 %collective-permute-start.5 = (bf16[512,768]{1,0:T(8,128)(2,1)S(1)}, bf16[512,768]{1,0:T(8,128)(2,1)S(1)}, u32[]{:S(2)}, u32[]{:S(2)}) collective-permute-start(bf16[512,768]{1,0:T(8,128)(2,1)S(1)} %get-tuple-element.2), channel_id=1, source_target_pairs={{0,32},{32,0},{1,33},{33,1},{2,34},{34,2},{3,35},{35,3},{4,36},{36... | collective-permute-start | bytes 2359304 | tf_op jit(solution)/shard_map/ppermute | solution.py:46
  (3 other events, 8.9 us)
Sparse Core Ops, SparseCore 0:
  11.7 71.0 all-gather.2
  84.5 39.3 all-gather.4
  276.5 41.0 reduce-scatter.4
  320.0 41.5 reduce-scatter.2
